TPU v7x, 32 devices: a whole 2x2x4 slice. The times are simulated.
32 devices in a mesh: blk: 16 (over z, y, x), col: 2 (over core).
Axes of the slice: x: 2, y: 2, z: 4, core: 2. Of those that a mesh axis runs over, the one named last changes fastest.
Arguments:
- trial: bfloat16 [32768, 128], P(('blk', 'col')), may hold values from -6 to 6
- omega: float32 [32768], P(('blk', 'col')), may hold values from 0.5 to 6
- table: bfloat16 [64, 128, 128], replicated, may hold values from -0.0625 to 0.0625
- block_type: int32 [256, 72], P(('blk', 'col')), may hold values from 0 to 63
- cycle_offset: int32 [256, 72], P(('blk', 'col')), may hold values from -4 to 4
- source_block: int32 [256, 72], P(('blk', 'col')), may hold values from 0 to 7
Outputs:
- sigma: bfloat16 [32768, 128], P(('blk', 'col'))
- projected: float32 [128, 128], replicated
- basis: float32 [32768, 128], P(('blk', 'col'))
All inputs are finite; a program needn't handle non-finite values.
Results may differ from a plain program's by a relative error of at most 0.006.
Values may be sent and summed in bfloat16 or wider, within the bound.
A program may use at most 64 MiB of HBM per device.

v0:
```python
import jax
import jax.numpy as jnp
from jax import lax
from jax.sharding import PartitionSpec as P

REACH = 4


def from_behind(value, axis, steps):
    count = lax.axis_size(axis)
    pairs = [(source, (source + steps) % count) for source in range(count)]
    return lax.ppermute(value, axis, pairs)


def on_device(trial, omega, table, block_type, cycle_offset, source_block):
    row_count = trial.shape[0]
    vec_count = trial.shape[1]
    pair_block = table.shape[1]
    blocks = row_count // pair_block
    own_slab = trial.reshape(blocks, pair_block, vec_count)
    slabs = {0: own_slab}
    offsets = [offset for offset in range(0 - REACH, REACH + 1) if offset != 0]
    for offset in offsets:
        slabs[offset] = from_behind(own_slab, "blk", 0 - offset)
    stacked = jnp.stack([slabs[offset] for offset in range(0 - REACH, REACH + 1)])
    stacked = stacked.reshape((2 * REACH + 1) * blocks, pair_block, vec_count)
    tile_index = (cycle_offset + REACH) * blocks + source_block
    energy = omega.reshape(blocks, pair_block)

    def one_block(operands):
        kinds, chosen, energy_row, own_rows = operands
        sources = stacked[chosen]
        coeffs = table[kinds]
        coupled = jnp.einsum("jab,jbk->ak", coeffs, sources, preferred_element_type=jnp.float32)
        return (coupled + energy_row[:, None] * own_rows.astype(jnp.float32)).astype(jnp.bfloat16)

    sigma = lax.map(one_block, (block_type, tile_index, energy, own_slab)).reshape(
        row_count, vec_count
    )
    highest = lax.Precision.HIGHEST
    sigma_full = sigma.astype(jnp.float32)
    trial_full = trial.astype(jnp.float32)
    total = row_count * lax.axis_size("blk") * lax.axis_size("col")
    projected = (
        lax.psum(jnp.dot(trial_full.T, sigma_full, precision=highest), ("blk", "col")) / total
    )
    residual = sigma_full - jnp.dot(trial_full, projected, precision=highest)
    gram = lax.psum(jnp.dot(residual.T, residual, precision=highest), ("blk", "col")) / total
    lower = jnp.linalg.cholesky(gram)
    inverse = jax.scipy.linalg.solve_triangular(
        lower, jnp.eye(vec_count, dtype=jnp.float32), lower=True
    )
    basis = jnp.dot(residual, inverse.T, precision=highest)
    return (sigma, projected, basis)


def solution(mesh):
    placed = (
        P(("blk", "col"), None),
        P(("blk", "col")),
        P(),
        P(("blk", "col"), None),
        P(("blk", "col"), None),
        P(("blk", "col"), None),
    )
    return jax.shard_map(
        on_device,
        mesh=mesh,
        in_specs=placed,
        out_specs=(P(("blk", "col"), None), P(), P(("blk", "col"), None)),
        check_vma=False,
    )
```

profile of v0, /device:TPU:0, one launch (start us, length us, event | category | flops | bytes accessed | tf_op | source)
XLA Modules:
  0.0 411.2 jit_solution(719922442792126760)
XLA Ops:
  7.2 3.1 collective-permute-start
  10.3 2.4 collective-permute-start.1
  12.7 1.5 collective-permute-start.2
  14.8 5.0 %collective-permute-start.4 = (bf16[8,128,128]{2,1,0:T(8,128)(2,1)}, bf16[8,128,128]{2,1,0:T(8,128)(2,1)S(1)}, u32[]{:S(2)}, u32[]{:S(2)}) collective-permute-start(bf16[8,128,128]{2,1,0:T(8,128)(2,1)} %bitcast.101), channel_id=1, source_target_pairs={{0,30},{2,0},{4,2},{6,4},{8,6},{10,8},{12,10},{14,12},{16,14},{18,... | collective-permute-start | bytes 786440 | tf_op jit(solution)/shard_map/ppermute | solution.py:12
  19.9 0.7 multiply_add_fusion
  20.6 2.1 collective-permute-start.5
  22.7 3.8 collective-permute-done.1
  26.5 3.2 collective-permute-start.6
  29.7 3.6 collective-permute-done.2
  33.3 11.1 %collective-permute-start.7 = (bf16[8,128,128]{2,1,0:T(8,128)(2,1)}, bf16[8,128,128]{2,1,0:T(8,128)(2,1)S(1)}, u32[]{:S(2)}, u32[]{:S(2)}) collective-permute-start(bf16[8,128,128]{2,1,0:T(8,128)(2,1)} %bitcast.104), channel_id=1, source_target_pairs={{0,24},{2,26},{4,28},{6,30},{8,0},{10,2},{12,4},{14,6},{16,8},{18,... | collective-permute-start | bytes 786440 | tf_op jit(solution)/shard_map/ppermute | solution.py:12
  44.5 1.0 constant_dynamic-update-slice_fusion
  45.6 3.0 collective-permute-done.7
  48.6 1.4 copy-done
  50.0 84.5 %while.10 = (s32[]{:T(128)}, bf16[8,128,128]{2,1,0:T(8,128)(2,1)S(1)}, s32[8,72]{1,0:T(8,128)}, bf16[64,128,128]{2,1,0:T(8,128)(2,1)}, s32[8,72]{1,0:T(8,128)S(1...) while((s32[]{:T(128)}, ...), condition=%wide.region_1.2_spmd, body=%wide.region_0.1_spmd.sunk | while | flops 302057920 | bytes 14233449 | solution.py:37
  50.0 0.7 fusion.32
  50.7 2.6 gather_fusion
  53.3 4.1 gather_fusion.1
  57.4 0.7 fusion.33
  58.1 2.4 fusion.34
  60.6 0.7 fusion.32
  61.3 2.6 gather_fusion
  63.9 4.1 gather_fusion.1
  68.0 0.7 fusion.33
  68.7 2.4 fusion.34
  71.2 0.7 fusion.32
  71.9 2.6 gather_fusion
  74.5 4.1 gather_fusion.1
  78.6 0.7 fusion.33
  79.3 2.4 fusion.34
  81.7 0.7 fusion.32
  82.4 2.6 gather_fusion
  85.0 4.1 gather_fusion.1
  89.1 0.7 fusion.33
  89.8 2.4 fusion.34
  92.3 0.7 fusion.32
  93.0 2.6 gather_fusion
  95.6 4.1 gather_fusion.1
  99.7 0.7 fusion.33
  100.4 2.4 fusion.34
  102.9 0.7 fusion.32
  103.6 2.6 gather_fusion
  106.2 4.1 gather_fusion.1
  110.3 0.7 fusion.33
  111.0 2.4 fusion.34
  113.4 0.7 fusion.32
  114.1 2.6 gather_fusion
  116.7 4.1 gather_fusion.1
  121.5 2.4 fusion.34
  124.0 0.7 fusion.32
  124.7 2.6 gather_fusion
  127.3 4.1 gather_fusion.1
  132.1 2.4 fusion.34
  134.6 0.9 convolution_bitcast_fusion.2
  135.7 117.4 %all-reduce.3.cloned.1.call-done = f32[128,128]{0,1:T(8,128)} async-done(((f32[128,128]{0,1:T(8,128)}), f32[128,128]{0,1:T(8,128)}) %all-reduce.3.cloned.1.call-update) | async-done | bytes 65552 | tf_op jit(solution)/shard_map/psum | solution.py:45
  253.1 1.2 fusion.9
  254.3 1.2 fusion.14
  255.6 0.8 broadcast_multiply_fusion.1
  256.4 0.7 copy.13
  257.1 120.5 %all-reduce.5.cloned.1.call-done = f32[128,128]{0,1:T(8,128)} async-done(((f32[128,128]{0,1:T(8,128)}), f32[128,128]{0,1:T(8,128)}) %all-reduce.5.cloned.1.call-update) | async-done | bytes 65552 | tf_op jit(solution)/shard_map/psum | solution.py:48
  377.6 0.8 broadcast_multiply_fusion
  378.6 0.9 fusion.13
  379.4 11.7 %cholesky.17 = f32[128,128]{1,0:T(8,128)S(1)} custom-call(f32[128,128]{1,0:T(8,128)S(1)} %fusion.13), custom_call_target="Cholesky" | custom-call | tf_op jit(solution)/shard_map/jit(cholesky)/cholesky | solution.py:49
  392.5 9.8 %custom-call.7 = f32[1,128,128]{1,2,0:T(8,128)S(1)} custom-call(f32[1,128,128]{2,1,0:T(8,128)S(1)} %fusion.10), custom_call_target="InvertDiagBlocksLowerTriangular" | custom-call | tf_op jit(solution)/shard_map/jit(_solve_triangular)/triangular_solve | solution.py:50
  402.5 1.8 fusion.15
  (48 shorter events, 4.3 us)
Async XLA Ops:
  7.2 245.9 %all-reduce.3.cloned.1.call-start = ((), (), s32[]{:S(2)}) async-start(), calls=%async_computation | async-start | bytes 131072 | tf_op jit(solution)/shard_map/psum | solution.py:45
  7.2 13.4 %collective-permute-start = (bf16[8,128,128]{2,1,0:T(8,128)(2,1)}, bf16[8,128,128]{2,1,0:T(8,128)(2,1)S(1)}, u32[]{:S(2)}, u32[]{:S(2)}) collective-permute-start(bf16[8,128,128]{2,1,0:T(8,128)(2,1)} %bitcast.97), channel_id=1, source_target_pairs={{0,8},{2,10},{4,12},{6,14},{8,16},{10,18},{12,20},{14,22},{16,24},... | collective-permute-start | bytes 786440 | tf_op jit(solution)/shard_map/ppermute | solution.py:12
  10.3 16.2 %collective-permute-start.1 = (bf16[8,128,128]{2,1,0:T(8,128)(2,1)}, bf16[8,128,128]{2,1,0:T(8,128)(2,1)S(1)}, u32[]{:S(2)}, u32[]{:S(2)}) collective-permute-start(bf16[8,128,128]{2,1,0:T(8,128)(2,1)} %bitcast.98), channel_id=1, source_target_pairs={{0,6},{2,8},{4,10},{6,12},{8,14},{10,16},{12,18},{14,20},{16,22},{... | collective-permute-start | bytes 786440 | tf_op jit(solution)/shard_map/ppermute | solution.py:12
  12.7 20.6 %collective-permute-start.2 = (bf16[8,128,128]{2,1,0:T(8,128)(2,1)}, bf16[8,128,128]{2,1,0:T(8,128)(2,1)S(1)}, u32[]{:S(2)}, u32[]{:S(2)}) collective-permute-start(bf16[8,128,128]{2,1,0:T(8,128)(2,1)} %bitcast.99), channel_id=1, source_target_pairs={{0,4},{2,6},{4,8},{6,10},{8,12},{10,14},{12,16},{14,18},{16,20},{1... | collective-permute-start | bytes 786440 | tf_op jit(solution)/shard_map/ppermute | solution.py:12
  14.3 30.2 %collective-permute-start.3 = (bf16[8,128,128]{2,1,0:T(8,128)(2,1)}, bf16[8,128,128]{2,1,0:T(8,128)(2,1)S(1)}, u32[]{:S(2)}, u32[]{:S(2)}) collective-permute-start(bf16[8,128,128]{2,1,0:T(8,128)(2,1)} %bitcast.100), channel_id=1, source_target_pairs={{0,2},{2,4},{4,6},{6,8},{8,10},{10,12},{12,14},{14,16},{16,18},{18... | collective-permute-start | bytes 786440 | tf_op jit(solution)/shard_map/ppermute | solution.py:12
  14.8 30.6 %collective-permute-start.4 = (bf16[8,128,128]{2,1,0:T(8,128)(2,1)}, bf16[8,128,128]{2,1,0:T(8,128)(2,1)S(1)}, u32[]{:S(2)}, u32[]{:S(2)}) collective-permute-start(bf16[8,128,128]{2,1,0:T(8,128)(2,1)} %bitcast.101), channel_id=1, source_target_pairs={{0,30},{2,0},{4,2},{6,4},{8,6},{10,8},{12,10},{14,12},{16,14},{18,... | collective-permute-start | bytes 786440 | tf_op jit(solution)/shard_map/ppermute | solution.py:12
  20.6 29.4 %copy-start.1 = (bf16[1024,128]{1,0:T(8,128)(2,1)S(1)}, bf16[1024,128]{1,0:T(8,128)(2,1)}, u32[]{:S(2)}) copy-start(bf16[1024,128]{1,0:T(8,128)(2,1)} %param.8) | copy-start | bytes 786436
  20.6 24.9 %collective-permute-start.5 = (bf16[8,128,128]{2,1,0:T(8,128)(2,1)}, bf16[8,128,128]{2,1,0:T(8,128)(2,1)S(1)}, u32[]{:S(2)}, u32[]{:S(2)}) collective-permute-start(bf16[8,128,128]{2,1,0:T(8,128)(2,1)} %bitcast.102), channel_id=1, source_target_pairs={{0,28},{2,30},{4,0},{6,2},{8,4},{10,6},{12,8},{14,10},{16,12},{18,... | collective-permute-start | bytes 786440 | tf_op jit(solution)/shard_map/ppermute | solution.py:12
  26.5 19.1 %collective-permute-start.6 = (bf16[8,128,128]{2,1,0:T(8,128)(2,1)}, bf16[8,128,128]{2,1,0:T(8,128)(2,1)S(1)}, u32[]{:S(2)}, u32[]{:S(2)}) collective-permute-start(bf16[8,128,128]{2,1,0:T(8,128)(2,1)} %bitcast.103), channel_id=1, source_target_pairs={{0,26},{2,28},{4,30},{6,0},{8,2},{10,4},{12,6},{14,8},{16,10},{18,... | collective-permute-start | bytes 786440 | tf_op jit(solution)/shard_map/ppermute | solution.py:12
  33.3 15.3 %collective-permute-start.7 = (bf16[8,128,128]{2,1,0:T(8,128)(2,1)}, bf16[8,128,128]{2,1,0:T(8,128)(2,1)S(1)}, u32[]{:S(2)}, u32[]{:S(2)}) collective-permute-start(bf16[8,128,128]{2,1,0:T(8,128)(2,1)} %bitcast.104), channel_id=1, source_target_pairs={{0,24},{2,26},{4,28},{6,30},{8,0},{10,2},{12,4},{14,6},{16,8},{18,... | collective-permute-start | bytes 786440 | tf_op jit(solution)/shard_map/ppermute | solution.py:12
  48.6 1.4 copy-start
  134.6 269.8 %copy-start.2 = (bf16[8,128,128]{2,1,0:T(8,128)(2,1)}, bf16[8,128,128]{2,1,0:T(8,128)(2,1)S(1)}, u32[]{:S(2)}) copy-start(bf16[8,128,128]{2,1,0:T(8,128)(2,1)S(1)} %get-tuple-element.45) | copy-start | bytes 786436
  135.5 242.1 %all-reduce.5.cloned.1.call-start = ((), (), s32[]{:S(2)}) async-start(), calls=%async_computation.1 | async-start | bytes 131072 | tf_op jit(solution)/shard_map/psum | solution.py:48
Sparse Core Ops, SparseCore 0:
  135.6 117.4 all-reduce.2
  259.2 118.3 all-reduce.4
where the time goes:
time: 414 us; the launch traced here: 411 us
  waiting for transfers between devices  248 us (60%)
  local copies, waits for them, and re-layouts  62.7 us (15%)
  other arithmetic  31.8 us (8%)
  starting transfers between devices  29.1 us (7%)
  matrix products  24.9 us (6%)
  between operations  14.2 us (3%)
    psum x1, waiting for transfers between devices, on_device(): lax.psum(jnp.dot(residual.T, residual, precision=highest), ('blk', 'col'))  120 us
    psum x1, waiting for transfers between devices, on_device(): lax.psum(jnp.dot(trial_full.T, sigma_full, precision=highest), ('blk', 'c...  117 us
    gather x8, local copies, waits for them, and re-layouts, one_block(): sources = stacked[chosen]  32.8 us
    ppermute x8, starting transfers between devices, from_behind(): return lax.ppermute(value, axis, pairs)  29 us
    gather x8, local copies, waits for them, and re-layouts, one_block(): coeffs = table[kinds]  20.7 us
    dot_general x8, matrix products, one_block(): jnp.einsum('jab,jbk->ak', coeffs, sources, preferred_element_type=jnp.flo...  19.6 us
    another operation x3, other arithmetic, on_device(): lower = jnp.linalg.cholesky(gram)  12.4 us
    another operation x2, other arithmetic, on_device(): jax.scipy.linalg.solve_triangular(lower, jnp.eye(vec_count, dtype=jnp.flo...  10.5 us
  transfers between devices with their start and end apart: 10, of which 5 were waited for; matrix products, arithmetic and copies ran while one was open for 1% of the time, Pallas kernels for 0%

commit v1 on v0

v1 whole, which is shorter than its diff:
```python
import functools

import jax
import jax.numpy as jnp
from jax import lax
from jax.experimental import pallas as pl
from jax.experimental.pallas import tpu as pltpu
from jax.sharding import PartitionSpec as P

REACH = 4
MESH = pl.DeviceIdType.MESH
HIGHEST = lax.Precision.HIGHEST
OFFSETS = [sign * step for step in range(REACH, 0, -1) for sign in (1, -1)]


def wrap(index, count):
    return lax.rem(index + count, count)


def dot_tn(left, right):
    return lax.dot_general(
        left, right, (((0,), (0,)), ((), ())), preferred_element_type=jnp.float32
    )


def couple_kernel(
    n_blk, n_col, near, kinds_ref, chosen_ref, trial_ref, omega_ref, table_hbm,
    sigma_ref, sums_ref,
    table_ref, slabs, part, gathered, ring, total,
    local_sems, g_send, g_recv, r_send, r_recv, z_send, z_recv, a_send, a_recv,
):
    blocks, pair_block, vec_count = trial_ref.shape
    per_row = kinds_ref.shape[1]
    rows = part.shape[0]
    me_b = lax.axis_index("blk")
    me_c = lax.axis_index("col")
    group = near * n_col
    far = n_blk // near
    piece = rows // group
    low = lax.rem(me_b, near)
    high = me_b // near
    mine = low * n_col + me_c

    def near_id(index):
        return (high * near + index // n_col, lax.rem(index, n_col))

    def far_id(index):
        return (index * near + low, me_c)

    load_table = pltpu.make_async_copy(table_hbm, table_ref, local_sems.at[0])
    load_table.start()
    keep_own = pltpu.make_async_copy(trial_ref, slabs.at[REACH], local_sems.at[1])
    keep_own.start()

    barrier = pltpu.get_barrier_semaphore()
    for offset in OFFSETS:
        pl.semaphore_signal(
            barrier, inc=1, device_id=(wrap(me_b - offset, n_blk), me_c), device_id_type=MESH
        )
    for step in range(1, group):
        pl.semaphore_signal(
            barrier, inc=1, device_id=near_id(wrap(mine + step, group)), device_id_type=MESH
        )
    for step in range(1, far):
        pl.semaphore_signal(
            barrier, inc=1, device_id=far_id(wrap(high + step, far)), device_id_type=MESH
        )
    pl.semaphore_wait(barrier, len(OFFSETS) + group - 1 + far - 1)

    sends = []
    for number, offset in enumerate(OFFSETS):
        copy = pltpu.make_async_remote_copy(
            src_ref=trial_ref,
            dst_ref=slabs.at[offset + REACH],
            send_sem=g_send.at[number],
            recv_sem=g_recv.at[number],
            device_id=(wrap(me_b - offset, n_blk), me_c),
            device_id_type=MESH,
        )
        copy.start()
        sends.append(copy)

    own = trial_ref[...].reshape(blocks * pair_block, vec_count)
    part[0:vec_count, :] = dot_tn(own, own)
    load_table.wait()
    keep_own.wait()
    for copy in sends:
        copy.wait()

    chunk = max(size for size in range(1, 9) if per_row % size == 0)
    row_id = lax.broadcasted_iota(jnp.int32, (pair_block, pair_block), 0)
    lane_id = lax.broadcasted_iota(jnp.int32, (pair_block, pair_block), 1)

    def one_block(r, carry):
        energy = jnp.broadcast_to(omega_ref[pl.ds(r, 1), :], (pair_block, pair_block))
        column = jnp.sum(jnp.where(row_id == lane_id, energy, 0.0), axis=1, keepdims=True)
        acc = column * trial_ref[r].astype(jnp.float32)
        for start in range(0, per_row, chunk):
            coeffs = []
            sources = []
            for j in range(start, start + chunk):
                coeffs.append(table_ref[kinds_ref[r, j]])
                tile = chosen_ref[r, j]
                sources.append(slabs[tile // blocks, lax.rem(tile, blocks)])
            acc = acc + jnp.dot(
                jnp.concatenate(coeffs, axis=1),
                jnp.concatenate(sources, axis=0),
                preferred_element_type=jnp.float32,
            )
        sigma_ref[pl.ds(pl.multiple_of(r * pair_block, pair_block), pair_block), :] = acc.astype(
            jnp.bfloat16
        )
        return carry

    lax.fori_loop(0, blocks, one_block, 0)

    sigma = sigma_ref[...]
    both = jnp.concatenate([own, sigma], axis=1)
    part[vec_count : 3 * vec_count, :] = dot_tn(both, sigma)

    copies = []
    for step in range(1, group):
        peer = wrap(mine + step, group)
        copy = pltpu.make_async_remote_copy(
            src_ref=part.at[pl.ds(pl.multiple_of(peer * piece, 8), piece)],
            dst_ref=gathered.at[step - 1],
            send_sem=r_send.at[step - 1],
            recv_sem=r_recv.at[step - 1],
            device_id=near_id(peer),
            device_id_type=MESH,
        )
        copy.start()
        copies.append(copy)
    piece_sum = part[pl.ds(pl.multiple_of(mine * piece, 8), piece), :]
    for step, copy in enumerate(copies):
        copy.wait()
        piece_sum = piece_sum + gathered[step]
    ring[high] = piece_sum

    copies = []
    for step in range(1, far):
        copy = pltpu.make_async_remote_copy(
            src_ref=ring.at[high],
            dst_ref=ring.at[high],
            send_sem=z_send.at[step - 1],
            recv_sem=z_recv.at[step - 1],
            device_id=far_id(wrap(high + step, far)),
            device_id_type=MESH,
        )
        copy.start()
        copies.append(copy)
    for copy in copies:
        copy.wait()
    piece_sum = ring[0]
    for index in range(1, far):
        piece_sum = piece_sum + ring[index]
    my_rows = pl.ds(pl.multiple_of(mine * piece, 8), piece)
    total[my_rows, :] = piece_sum

    copies = []
    for step in range(1, group):
        copy = pltpu.make_async_remote_copy(
            src_ref=total.at[my_rows],
            dst_ref=total.at[my_rows],
            send_sem=a_send.at[step - 1],
            recv_sem=a_recv.at[step - 1],
            device_id=near_id(wrap(mine + step, group)),
            device_id_type=MESH,
        )
        copy.start()
        copies.append(copy)
    for copy in copies:
        copy.wait()
    sums_ref[...] = total[...]


def split_three(value):
    high = value.astype(jnp.bfloat16)
    rest = value - high.astype(jnp.float32)
    middle = rest.astype(jnp.bfloat16)
    low = (rest - middle.astype(jnp.float32)).astype(jnp.bfloat16)
    return high, middle, low


def inverse_factor(gram):
    size = gram.shape[0]
    tiles = [gram[8 * t : 8 * t + 8, :] for t in range(size // 8)]
    lane = lax.broadcasted_iota(jnp.int32, (8, size), 1)
    sub = lax.broadcasted_iota(jnp.int32, (8, size), 0)
    for j in range(size):
        own, inner = j // 8, j % 8
        here = lane == j
        row = jnp.broadcast_to(tiles[own][inner : inner + 1, :], (8, size))
        pivot = jnp.broadcast_to(row[:, j : j + 1], (8, size))
        scaled = jnp.where(here, 1.0, row) * (1.0 / pivot)
        for t in range(own, size // 8):
            if t == own and inner == 7:
                continue
            column = jnp.broadcast_to(tiles[t][:, j : j + 1], (8, size))
            updated = jnp.where(here, 0.0, tiles[t]) - column * scaled
            tiles[t] = jnp.where(sub > inner, updated, tiles[t]) if t == own else updated
    inverse = []
    for t in range(size // 8):
        diagonal = lane == sub + 8 * t
        pivots = jnp.sum(jnp.where(diagonal, tiles[t], 0.0), axis=1, keepdims=True)
        unit = jnp.where(diagonal, 1.0, jnp.where(lane < sub + 8 * t, tiles[t], 0.0))
        inverse.append(unit / jnp.sqrt(pivots))
    return jnp.concatenate(inverse, axis=0)


def basis_kernel(total_rows, sums_ref, trial_ref, sigma_ref, projected_ref, basis_ref):
    size = sums_ref.shape[1]
    scale = 1.0 / total_rows
    overlap = sums_ref[0:size, :] * scale
    projected = sums_ref[size : 2 * size, :] * scale
    projected_ref[...] = projected
    square = sums_ref[2 * size : 3 * size, :] * scale
    row = lax.broadcasted_iota(jnp.int32, (size, size), 0)
    lane = lax.broadcasted_iota(jnp.int32, (size, size), 1)
    middle = jnp.where(row == lane, 2.0, 0.0) - overlap
    folded = jnp.dot(middle, projected, precision=HIGHEST, preferred_element_type=jnp.float32)
    gram = square - lax.dot_general(
        projected, folded, (((0,), (0,)), ((), ())),
        precision=HIGHEST, preferred_element_type=jnp.float32,
    )
    inverse = inverse_factor(gram)
    upper = inverse.T
    pulled = jnp.dot(projected, upper, precision=HIGHEST, preferred_element_type=jnp.float32)
    weights = jnp.concatenate([upper, 0.0 - pulled], axis=0)
    both = jnp.concatenate([sigma_ref[...], trial_ref[...]], axis=1)
    result = None
    for term in reversed(split_three(weights)):
        product = jnp.dot(both, term, preferred_element_type=jnp.float32)
        result = product if result is None else result + product
    basis_ref[...] = result


def on_device(n_blk, n_col, trial, omega, table, block_type, cycle_offset, source_block):
    row_count, vec_count = trial.shape
    pair_block = table.shape[1]
    blocks = row_count // pair_block
    near = max(size for size in (4, 2, 1) if n_blk % size == 0)
    group = near * n_col
    far = n_blk // near
    rows = 3 * vec_count
    piece = rows // group
    tile_index = (cycle_offset + REACH) * blocks + source_block
    vmem = pl.BlockSpec(memory_space=pltpu.VMEM)
    smem = pl.BlockSpec(memory_space=pltpu.SMEM)
    dma = pltpu.SemaphoreType.DMA
    sigma, sums = pl.pallas_call(
        functools.partial(couple_kernel, n_blk, n_col, near),
        out_shape=(
            jax.ShapeDtypeStruct((row_count, vec_count), jnp.bfloat16),
            jax.ShapeDtypeStruct((rows, vec_count), jnp.float32),
        ),
        in_specs=[smem, smem, vmem, vmem, pl.BlockSpec(memory_space=pl.ANY)],
        out_specs=(vmem, vmem),
        scratch_shapes=[
            pltpu.VMEM(table.shape, jnp.bfloat16),
            pltpu.VMEM((2 * REACH + 1, blocks, pair_block, vec_count), jnp.bfloat16),
            pltpu.VMEM((rows, vec_count), jnp.float32),
            pltpu.VMEM((group - 1, piece, vec_count), jnp.float32),
            pltpu.VMEM((far, piece, vec_count), jnp.float32),
            pltpu.VMEM((rows, vec_count), jnp.float32),
            dma((2,)),
            dma((2 * REACH,)),
            dma((2 * REACH,)),
            dma((group - 1,)),
            dma((group - 1,)),
            dma((far - 1,)),
            dma((far - 1,)),
            dma((group - 1,)),
            dma((group - 1,)),
        ],
        compiler_params=pltpu.CompilerParams(
            collective_id=0, has_side_effects=True, vmem_limit_bytes=32 << 20
        ),
        name="couple",
    )(
        block_type,
        tile_index,
        trial.reshape(blocks, pair_block, vec_count),
        omega.reshape(blocks, pair_block),
        table,
    )
    projected, basis = pl.pallas_call(
        functools.partial(basis_kernel, row_count * n_blk * n_col),
        out_shape=(
            jax.ShapeDtypeStruct((vec_count, vec_count), jnp.float32),
            jax.ShapeDtypeStruct((row_count, vec_count), jnp.float32),
        ),
        in_specs=[vmem] * 3,
        out_specs=(vmem, vmem),
        compiler_params=pltpu.CompilerParams(vmem_limit_bytes=32 << 20),
        name="basis",
    )(sums, trial, sigma)
    return (sigma, projected, basis)


def solution(mesh):
    placed = (
        P(("blk", "col"), None),
        P(("blk", "col")),
        P(),
        P(("blk", "col"), None),
        P(("blk", "col"), None),
        P(("blk", "col"), None),
    )
    return jax.shard_map(
        functools.partial(on_device, mesh.shape["blk"], mesh.shape["col"]),
        mesh=mesh,
        in_specs=placed,
        out_specs=(P(("blk", "col"), None), P(), P(("blk", "col"), None)),
        check_vma=False,
    )
```

time: 414 us -> 88.3 us (0.21)
  waiting for transfers between devices: 248 us -> 0 us
  Pallas kernels: 0 us -> 82 us
  local copies, waits for them, and re-layouts: 62.7 us -> 4.62 us
  other arithmetic: 31.8 us -> 0.71 us
  starting transfers between devices: 29.1 us -> 0 us
  matrix products: 24.9 us -> 0 us
  between operations: 14.2 us -> 0.65 us
    psum x2 -> x0, waiting for transfers between devices: 238 us -> none  [the longest x1 120 us: on_device(): lax.psum(jnp.dot(residual.T, residual, precision=highest), ('blk', 'col'))]
    pallas_call x0 -> x2, Pallas kernels: none -> 82 us  [the longest x1 62.6 us: on_device(): pl.pallas_call(functools.partial(couple_kernel, n_blk, n_col, near), out_...]
    gather x16 -> x0, local copies, waits for them, and re-layouts: 53.5 us -> none  [the longest x8 32.8 us: one_block(): sources = stacked[chosen]]
    ppermute x8 -> x0, starting transfers between devices: 29 us -> none  [from_behind(): return lax.ppermute(value, axis, pairs)]
    dot_general x12 -> x0, matrix products: 24.7 us -> none  [the longest x8 19.6 us: one_block(): jnp.einsum('jab,jbk->ak', coeffs, sources, preferred_element_type=jnp.flo...]
    another operation x5 -> x0, other arithmetic: 22.9 us -> none  [the longest x3 12.4 us: on_device(): lower = jnp.linalg.cholesky(gram)]
    ppermute x8 -> x0, waiting for transfers between devices: 10.3 us -> none  [from_behind(): return lax.ppermute(value, axis, pairs)]
    select_n x8 -> x0, other arithmetic: 5.58 us -> none  [one_block(): coeffs = table[kinds]]
  transfers between devices with their start and end apart: 10 -> 0, of which waited for: 5 -> 0; matrix products, arithmetic and copies ran while one was open for 1% -> 0% of each run, Pallas kernels for 0% -> 0%
where the time goes in v1:
time: 88.3 us; the launch traced here: 88 us
  Pallas kernels  82 us (93%)
  local copies, waits for them, and re-layouts  4.62 us (5%)
    pallas_call x1, Pallas kernels, on_device(): pl.pallas_call(functools.partial(couple_kernel, n_blk, n_col, near), out_...  62.6 us
    pallas_call x1, Pallas kernels, on_device(): pl.pallas_call(functools.partial(basis_kernel, row_count * n_blk * n_col)...  19.4 us
    unnamed x11, local copies, waits for them, and re-layouts  4.62 us

profile of v1, /device:TPU:0, one launch (start us, length us, event | category | flops | bytes accessed | tf_op | source)
XLA Modules:
  0.0 88.0 jit_solution(15532037671891338704)
XLA Ops:
  0.6 0.7 multiply_add_fusion.chosen_ref
  1.3 0.0 copy-start
  1.3 1.6 %copy-done = bf16[64,128,128]{2,1,0:T(8,128)(2,1)S(1)} copy-done((bf16[64,128,128]{2,1,0:T(8,128)(2,1)S(1)}, bf16[64,128,128]{2,1,0:T(8,128)(2,1)}, u32[]{:S(2)}) %copy-start) | copy-done | bytes 2097176
  2.9 0.0 copy-start.1
  2.9 0.9 %copy-done.1 = bf16[1024,128]{1,0:T(8,128)(2,1)S(1)} copy-done((bf16[1024,128]{1,0:T(8,128)(2,1)S(1)}, bf16[1024,128]{1,0:T(8,128)(2,1)}, u32[]{:S(2)}) %copy-start.1) | copy-done | bytes 262168
  3.9 0.0 copy-start.3
  3.9 0.7 copy-done.3
  4.6 0.0 copy-start.4
  4.6 0.7 copy-done.4
  5.3 0.0 copy-start.2
  5.3 62.6 %couple.1 = (bf16[1024,128]{1,0:T(8,128)(2,1)S(1)}, f32[384,128]{1,0:T(8,128)S(1)}) custom-call(s32[8,72]{1,0:T(8,128)S(1)} %copy-done.3, s32[8,72]{1,0:T(8,128)S(1)} %multiply_add_fusion.chosen_ref, bf16[8,128,128]{2,1,0:T(8,128)(2,1)S(1)} %bitcast.2, f32[8,128]{1,0:T(8,128)S(1)} %bitcast.3, bf16[64,128,128]{2,1,0:T(8,128)(2,1)S(1)} %copy-done), custom_call_target="tpu_custom_call" | custom-call | tf_op jit(solution)/shard_map/couple/pallas_call | solution.py:251
  67.9 0.0 copy-done.2
  67.9 19.4 %basis.1 = (f32[128,128]{1,0:T(8,128)}, f32[1024,128]{1,0:T(8,128)}) custom-call(f32[384,128]{1,0:T(8,128)S(1)} %get-tuple-element.8.sums_ref, bf16[1024,128]{1,0:T(8,128)(2,1)S(1)} %copy-done.2, bf16[1024,128]{1,0:T(8,128)(2,1)S(1)} %get-tuple-element.14.sigma_ref), custom_call_target="tpu_custom_call" | custom-call | tf_op jit(solution)/shard_map/basis/pallas_call | solution.py:287
  87.3 0.7 copy.10
Async XLA Ops:
  1.3 1.6 %copy-start = (bf16[64,128,128]{2,1,0:T(8,128)(2,1)S(1)}, bf16[64,128,128]{2,1,0:T(8,128)(2,1)}, u32[]{:S(2)}) copy-start(bf16[64,128,128]{2,1,0:T(8,128)(2,1)} %table_hbm.1) | copy-start | bytes 6291460
  2.9 0.9 %copy-start.1 = (bf16[1024,128]{1,0:T(8,128)(2,1)S(1)}, bf16[1024,128]{1,0:T(8,128)(2,1)}, u32[]{:S(2)}) copy-start(bf16[1024,128]{1,0:T(8,128)(2,1)} %trial_ref.1) | copy-start | bytes 786436
  3.9 0.7 copy-start.3
  4.6 0.7 copy-start.4
  5.3 62.6 %copy-start.2 = (bf16[1024,128]{1,0:T(8,128)(2,1)S(1)}, bf16[1024,128]{1,0:T(8,128)(2,1)}, u32[]{:S(2)}) copy-start(bf16[1024,128]{1,0:T(8,128)(2,1)} %trial_ref.1) | copy-start | bytes 786436

commit v2 on v1

--- a/solution.py
+++ b/solution.py
@@ -10,7 +10,7 @@
 REACH = 4
 MESH = pl.DeviceIdType.MESH
 HIGHEST = lax.Precision.HIGHEST
-OFFSETS = [sign * step for step in range(REACH, 0, -1) for sign in (1, -1)]
+PARTS = 2
 
 
 def wrap(index, count):
@@ -24,12 +24,13 @@
 
 
 def couple_kernel(
-    n_blk, n_col, near, kinds_ref, chosen_ref, trial_ref, omega_ref, table_hbm,
+    n_blk, n_col, near,
+    kinds_ref, cycle_ref, source_ref, trial_hbm, omega_hbm, table_hbm,
     sigma_ref, sums_ref,
-    table_ref, slabs, part, gathered, ring, total,
+    table_ref, slabs, omega_ref, part, gathered, ring, total,
     local_sems, g_send, g_recv, r_send, r_recv, z_send, z_recv, a_send, a_recv,
 ):
-    blocks, pair_block, vec_count = trial_ref.shape
+    blocks, pair_block, vec_count = trial_hbm.shape
     per_row = kinds_ref.shape[1]
     rows = part.shape[0]
     me_b = lax.axis_index("blk")
@@ -47,45 +48,104 @@
     def far_id(index):
         return (index * near + low, me_c)
 
-    load_table = pltpu.make_async_copy(table_hbm, table_ref, local_sems.at[0])
+    keep_own = pltpu.make_async_copy(trial_hbm, slabs.at[REACH], local_sems.at[0])
+    keep_own.start()
+    load_omega = pltpu.make_async_copy(omega_hbm, omega_ref, local_sems.at[1])
+    load_omega.start()
+    load_table = pltpu.make_async_copy(table_hbm, table_ref, local_sems.at[2])
     load_table.start()
-    keep_own = pltpu.make_async_copy(trial_ref, slabs.at[REACH], local_sems.at[1])
-    keep_own.start()
 
     barrier = pltpu.get_barrier_semaphore()
-    for offset in OFFSETS:
+    for step in range(1, far):
         pl.semaphore_signal(
-            barrier, inc=1, device_id=(wrap(me_b - offset, n_blk), me_c), device_id_type=MESH
+            barrier, inc=1, device_id=far_id(wrap(high + step, far)), device_id_type=MESH
         )
     for step in range(1, group):
         pl.semaphore_signal(
             barrier, inc=1, device_id=near_id(wrap(mine + step, group)), device_id_type=MESH
         )
-    for step in range(1, far):
-        pl.semaphore_signal(
-            barrier, inc=1, device_id=far_id(wrap(high + step, far)), device_id_type=MESH
-        )
-    pl.semaphore_wait(barrier, len(OFFSETS) + group - 1 + far - 1)
-
-    sends = []
-    for number, offset in enumerate(OFFSETS):
-        copy = pltpu.make_async_remote_copy(
-            src_ref=trial_ref,
-            dst_ref=slabs.at[offset + REACH],
-            send_sem=g_send.at[number],
-            recv_sem=g_recv.at[number],
-            device_id=(wrap(me_b - offset, n_blk), me_c),
+    pl.semaphore_wait(barrier, group - 1 + far - 1)
+
+    x = lax.rem(low, 2)
+    y = low // 2
+    up = wrap(me_b + REACH, n_blk)
+    down = wrap(me_b - REACH, n_blk)
+    side_x = me_b + 1 - 2 * x
+    side_y = me_b + 2 - 4 * y
+    span = blocks // PARTS
+
+    def message(number, h, source, slot, target):
+        rows_of = pl.ds(h * span, span)
+        return pltpu.make_async_remote_copy(
+            src_ref=trial_hbm.at[rows_of] if source is None else slabs.at[source, rows_of],
+            dst_ref=slabs.at[slot, rows_of],
+            send_sem=g_send.at[number, h],
+            recv_sem=g_recv.at[number, h],
+            device_id=(target, me_c),
             device_id_type=MESH,
         )
-        copy.start()
-        sends.append(copy)
-
-    own = trial_ref[...].reshape(blocks * pair_block, vec_count)
+
+    halves = range(PARTS)
+    to_up = [message(0, h, None, 0, up) for h in halves]
+    to_down = [message(1, h, None, 2 * REACH, down) for h in halves]
+    own_x = [message(2, h, None, 3 + 2 * x, side_x) for h in halves]
+    own_y = [message(3, h, None, 2 + 4 * y, side_y) for h in halves]
+    pass_y = [message(4, h, 5 - 2 * x, 3 - 2 * x + 4 * y, side_y) for h in halves]
+    far_x = [message(5, h, 8 - 8 * x, 7 - 6 * x, side_x) for h in halves]
+    far_y = [message(6, h, 8 - 8 * y, 6 - 4 * y, side_y) for h in halves]
+    pass_x = [message(7, h, 2 + 4 * y, 1 + 4 * y + 2 * x, side_x) for h in halves]
+
+    def far_arrival(bit, h):
+        return pltpu.make_async_remote_copy(
+            src_ref=trial_hbm.at[pl.ds(h * span, span)],
+            dst_ref=slabs.at[8 - 8 * bit, pl.ds(h * span, span)],
+            send_sem=g_send.at[1 - bit, h],
+            recv_sem=g_recv.at[1 - bit, h],
+            device_id=(up, me_c),
+            device_id_type=MESH,
+        )
+
+    for h in halves:
+        to_up[h].start()
+        to_down[h].start()
+        own_x[h].start()
+        own_y[h].start()
+
+    keep_own.wait()
+    own = slabs[REACH].reshape(blocks * pair_block, vec_count)
     part[0:vec_count, :] = dot_tn(own, own)
+
+    for h in halves:
+        own_x[h].wait_recv()
+        pass_y[h].start()
+    for h in halves:
+        far_arrival(x, h).wait_recv()
+        far_x[h].start()
+
+        @pl.when(x == y)
+        def _():
+            far_y[h].start()
+
+    for h in halves:
+        far_arrival(1 - x, h).wait_recv()
+
+        @pl.when(x != y)
+        def _():
+            far_y[h].start()
+
+    for h in halves:
+        far_y[h].wait_recv()
+        pass_x[h].start()
+    load_omega.wait()
     load_table.wait()
-    keep_own.wait()
-    for copy in sends:
-        copy.wait()
+    for h in halves:
+        own_y[h].wait_recv()
+        pass_y[h].wait_recv()
+        far_x[h].wait_recv()
+        pass_x[h].wait_recv()
+    for sent in (to_up, to_down, own_x, own_y, pass_y, far_x, far_y, pass_x):
+        for h in halves:
+            sent[h].wait_send()
 
     chunk = max(size for size in range(1, 9) if per_row % size == 0)
     row_id = lax.broadcasted_iota(jnp.int32, (pair_block, pair_block), 0)
@@ -94,14 +154,13 @@
     def one_block(r, carry):
         energy = jnp.broadcast_to(omega_ref[pl.ds(r, 1), :], (pair_block, pair_block))
         column = jnp.sum(jnp.where(row_id == lane_id, energy, 0.0), axis=1, keepdims=True)
-        acc = column * trial_ref[r].astype(jnp.float32)
+        acc = column * slabs[REACH, r].astype(jnp.float32)
         for start in range(0, per_row, chunk):
             coeffs = []
             sources = []
             for j in range(start, start + chunk):
                 coeffs.append(table_ref[kinds_ref[r, j]])
-                tile = chosen_ref[r, j]
-                sources.append(slabs[tile // blocks, lax.rem(tile, blocks)])
+                sources.append(slabs[cycle_ref[r, j] + REACH, source_ref[r, j]])
             acc = acc + jnp.dot(
                 jnp.concatenate(coeffs, axis=1),
                 jnp.concatenate(sources, axis=0),
@@ -184,21 +243,48 @@
 
 def inverse_factor(gram):
     size = gram.shape[0]
-    tiles = [gram[8 * t : 8 * t + 8, :] for t in range(size // 8)]
+    count = size // 8
+    tiles = [gram[8 * t : 8 * t + 8, :] for t in range(count)]
     lane = lax.broadcasted_iota(jnp.int32, (8, size), 1)
     sub = lax.broadcasted_iota(jnp.int32, (8, size), 0)
-    for j in range(size):
-        own, inner = j // 8, j % 8
-        here = lane == j
-        row = jnp.broadcast_to(tiles[own][inner : inner + 1, :], (8, size))
-        pivot = jnp.broadcast_to(row[:, j : j + 1], (8, size))
-        scaled = jnp.where(here, 1.0, row) * (1.0 / pivot)
-        for t in range(own, size // 8):
-            if t == own and inner == 7:
-                continue
-            column = jnp.broadcast_to(tiles[t][:, j : j + 1], (8, size))
-            updated = jnp.where(here, 0.0, tiles[t]) - column * scaled
-            tiles[t] = jnp.where(sub > inner, updated, tiles[t]) if t == own else updated
+
+    def spread_row(tile, k):
+        return jnp.broadcast_to(tile[k : k + 1, :], (8, size))
+
+    def spread_columns(tile, panel):
+        return [
+            jnp.broadcast_to(tile[:, 8 * panel + k : 8 * panel + k + 1], (8, size))
+            for k in range(8)
+        ]
+
+    for panel in range(count):
+        tile = tiles[panel]
+        columns = spread_columns(tile, panel)
+        later_rows = []
+        factors = []
+        for k in range(8):
+            here = lane == 8 * panel + k
+            reciprocal = 1.0 / spread_row(columns[k], k)
+            scaled = jnp.where(here, 1.0, spread_row(tile, k)) * reciprocal
+            later_rows.append(
+                jnp.where((lane > 8 * panel + k) & (lane < 8 * panel + 8), 0.0, scaled)
+            )
+            factors.append({m: spread_row(columns[m], k) * reciprocal for m in range(k + 1, 8)})
+            below = sub > k
+            lead = jnp.where(below, columns[k], 0.0)
+            tile = jnp.where(here & below, 0.0, tile) - lead * scaled
+            for m in range(k + 1, 8):
+                columns[m] = columns[m] - lead * factors[k][m]
+        tiles[panel] = tile
+        for t in range(panel + 1, count):
+            tile = tiles[t]
+            columns = spread_columns(tile, panel)
+            tile = jnp.where((lane >= 8 * panel) & (lane < 8 * panel + 8), 0.0, tile)
+            for k in range(8):
+                tile = tile - columns[k] * later_rows[k]
+                for m in range(k + 1, 8):
+                    columns[m] = columns[m] - columns[k] * factors[k][m]
+            tiles[t] = tile
     inverse = []
     for t in range(size // 8):
         diagonal = lane == sub + 8 * t
@@ -244,9 +330,9 @@
     far = n_blk // near
     rows = 3 * vec_count
     piece = rows // group
-    tile_index = (cycle_offset + REACH) * blocks + source_block
     vmem = pl.BlockSpec(memory_space=pltpu.VMEM)
     smem = pl.BlockSpec(memory_space=pltpu.SMEM)
+    hbm = pl.BlockSpec(memory_space=pltpu.HBM)
     dma = pltpu.SemaphoreType.DMA
     sigma, sums = pl.pallas_call(
         functools.partial(couple_kernel, n_blk, n_col, near),
@@ -254,18 +340,19 @@
             jax.ShapeDtypeStruct((row_count, vec_count), jnp.bfloat16),
             jax.ShapeDtypeStruct((rows, vec_count), jnp.float32),
         ),
-        in_specs=[smem, smem, vmem, vmem, pl.BlockSpec(memory_space=pl.ANY)],
+        in_specs=[smem, smem, smem, hbm, hbm, hbm],
         out_specs=(vmem, vmem),
         scratch_shapes=[
             pltpu.VMEM(table.shape, jnp.bfloat16),
             pltpu.VMEM((2 * REACH + 1, blocks, pair_block, vec_count), jnp.bfloat16),
+            pltpu.VMEM((blocks, pair_block), jnp.float32),
             pltpu.VMEM((rows, vec_count), jnp.float32),
             pltpu.VMEM((group - 1, piece, vec_count), jnp.float32),
             pltpu.VMEM((far, piece, vec_count), jnp.float32),
             pltpu.VMEM((rows, vec_count), jnp.float32),
-            dma((2,)),
-            dma((2 * REACH,)),
-            dma((2 * REACH,)),
+            dma((3,)),
+            dma((8, PARTS)),
+            dma((8, PARTS)),
             dma((group - 1,)),
             dma((group - 1,)),
             dma((far - 1,)),
@@ -274,12 +361,13 @@
             dma((group - 1,)),
         ],
         compiler_params=pltpu.CompilerParams(
-            collective_id=0, has_side_effects=True, vmem_limit_bytes=32 << 20
+            collective_id=0, has_side_effects=True, vmem_limit_bytes=60 << 20
         ),
         name="couple",
     )(
         block_type,
-        tile_index,
+        cycle_offset,
+        source_block,
         trial.reshape(blocks, pair_block, vec_count),
         omega.reshape(blocks, pair_block),
         table,
@@ -292,7 +380,7 @@
         ),
         in_specs=[vmem] * 3,
         out_specs=(vmem, vmem),
-        compiler_params=pltpu.CompilerParams(vmem_limit_bytes=32 << 20),
+        compiler_params=pltpu.CompilerParams(vmem_limit_bytes=60 << 20),
         name="basis",
     )(sums, trial, sigma)
     return (sigma, projected, basis)

time: 88.3 us -> 60.3 us (0.68)
  Pallas kernels: 82 us -> 57.8 us
  local copies, waits for them, and re-layouts: 4.62 us -> 1.67 us
    pallas_call x1, Pallas kernels: 62.6 us -> 50.4 us  [on_device(): pl.pallas_call(functools.partial(couple_kernel, n_blk, n_col, near), out_...]
    pallas_call x1, Pallas kernels: 19.4 us -> 7.42 us  [on_device(): pl.pallas_call(functools.partial(basis_kernel, row_count * n_blk * n_col)...]
    unnamed x11 -> x1, local copies, waits for them, and re-layouts: 4.62 us -> 1.67 us
where the time goes in v2:
time: 60.3 us; the launch traced here: 60.1 us
  Pallas kernels  57.8 us (96%)
  local copies, waits for them, and re-layouts  1.67 us (3%)
  between operations  0.64 us (1%)
    pallas_call x1, Pallas kernels, on_device(): pl.pallas_call(functools.partial(couple_kernel, n_blk, n_col, near), out_...  50.4 us
    pallas_call x1, Pallas kernels, on_device(): pl.pallas_call(functools.partial(basis_kernel, row_count * n_blk * n_col)...  7.42 us
    unnamed x1, local copies, waits for them, and re-layouts  1.67 us

profile of v2, /device:TPU:0, one launch (start us, length us, event | category | flops | bytes accessed | tf_op | source)
XLA Modules:
  0.0 60.1 jit_solution(5710965274254998097)
XLA Ops:
  0.6 50.4 %couple.1 = (bf16[1024,128]{1,0:T(8,128)(2,1)}, f32[384,128]{1,0:T(8,128)}) custom-call(s32[8,72]{1,0:T(8,128)} %kinds_ref.1, s32[8,72]{1,0:T(8,128)} %cycle_ref.1, s32[8,72]{1,0:T(8,128)} %source_ref.1, bf16[8,128,128]{2,1,0:T(8,128)(2,1)} %bitcast.2, f32[8,128]{1,0:T(8,128)} %bitcast.3, bf16[64,128,128]{2,1,0:T(8,128)(2,1)} %table_hbm.1), custom_call_target="tpu_custom_call" | custom-call | tf_op jit(solution)/shard_map/couple/pallas_call | solution.py:337
  51.1 7.4 %basis.1 = (f32[128,128]{1,0:T(8,128)}, f32[1024,128]{1,0:T(8,128)}) custom-call(f32[384,128]{1,0:T(8,128)} %get-tuple-element.8.sums_ref, bf16[1024,128]{1,0:T(8,128)(2,1)} %trial_ref.1, bf16[1024,128]{1,0:T(8,128)(2,1)} %get-tuple-element.14.sigma_ref), custom_call_target="tpu_custom_call" | custom-call | tf_op jit(solution)/shard_map/basis/pallas_call | solution.py:375
  58.5 1.7 %copy.10 = bf16[1024,128]{1,0:T(8,128)(2,1)} copy(bf16[1024,128]{1,0:T(8,128)(2,1)} %get-tuple-element.14.sigma_ref) | data formatting | bytes 524288

commit v3 on v2

--- a/solution.py
+++ b/solution.py
@@ -10,24 +10,18 @@
 REACH = 4
 MESH = pl.DeviceIdType.MESH
 HIGHEST = lax.Precision.HIGHEST
-PARTS = 2
+PARTS = 4
 
 
 def wrap(index, count):
     return lax.rem(index + count, count)
-
-
-def dot_tn(left, right):
-    return lax.dot_general(
-        left, right, (((0,), (0,)), ((), ())), preferred_element_type=jnp.float32
-    )
 
 
 def couple_kernel(
     n_blk, n_col, near,
     kinds_ref, cycle_ref, source_ref, trial_hbm, omega_hbm, table_hbm,
     sigma_ref, sums_ref,
-    table_ref, slabs, omega_ref, part, gathered, ring, total,
+    table_ref, slabs, across, omega_ref, part, gathered, ring, total,
     local_sems, g_send, g_recv, r_send, r_recv, z_send, z_recv, a_send, a_recv,
 ):
     blocks, pair_block, vec_count = trial_hbm.shape
@@ -113,7 +107,8 @@
 
     keep_own.wait()
     own = slabs[REACH].reshape(blocks * pair_block, vec_count)
-    part[0:vec_count, :] = dot_tn(own, own)
+    across[...] = own.T
+    part[0:vec_count, :] = jnp.dot(across[...], own, preferred_element_type=jnp.float32)
 
     for h in halves:
         own_x[h].wait_recv()
@@ -174,8 +169,10 @@
     lax.fori_loop(0, blocks, one_block, 0)
 
     sigma = sigma_ref[...]
-    both = jnp.concatenate([own, sigma], axis=1)
-    part[vec_count : 3 * vec_count, :] = dot_tn(both, sigma)
+    both = jnp.concatenate([across[...], sigma.T], axis=0)
+    part[vec_count : 3 * vec_count, :] = jnp.dot(
+        both, sigma, preferred_element_type=jnp.float32
+    )
 
     copies = []
     for step in range(1, group):
@@ -294,7 +291,9 @@
     return jnp.concatenate(inverse, axis=0)
 
 
-def basis_kernel(total_rows, sums_ref, trial_ref, sigma_ref, projected_ref, basis_ref):
+def basis_kernel(
+    total_rows, sums_ref, trial_ref, coupled_ref, sigma_ref, projected_ref, basis_ref
+):
     size = sums_ref.shape[1]
     scale = 1.0 / total_rows
     overlap = sums_ref[0:size, :] * scale
@@ -313,7 +312,9 @@
     upper = inverse.T
     pulled = jnp.dot(projected, upper, precision=HIGHEST, preferred_element_type=jnp.float32)
     weights = jnp.concatenate([upper, 0.0 - pulled], axis=0)
-    both = jnp.concatenate([sigma_ref[...], trial_ref[...]], axis=1)
+    coupled = coupled_ref[...]
+    sigma_ref[...] = coupled
+    both = jnp.concatenate([coupled, trial_ref[...]], axis=1)
     result = None
     for term in reversed(split_three(weights)):
         product = jnp.dot(both, term, preferred_element_type=jnp.float32)
@@ -334,7 +335,7 @@
     smem = pl.BlockSpec(memory_space=pltpu.SMEM)
     hbm = pl.BlockSpec(memory_space=pltpu.HBM)
     dma = pltpu.SemaphoreType.DMA
-    sigma, sums = pl.pallas_call(
+    coupled, sums = pl.pallas_call(
         functools.partial(couple_kernel, n_blk, n_col, near),
         out_shape=(
             jax.ShapeDtypeStruct((row_count, vec_count), jnp.bfloat16),
@@ -345,6 +346,7 @@
         scratch_shapes=[
             pltpu.VMEM(table.shape, jnp.bfloat16),
             pltpu.VMEM((2 * REACH + 1, blocks, pair_block, vec_count), jnp.bfloat16),
+            pltpu.VMEM((vec_count, row_count), jnp.bfloat16),
             pltpu.VMEM((blocks, pair_block), jnp.float32),
             pltpu.VMEM((rows, vec_count), jnp.float32),
             pltpu.VMEM((group - 1, piece, vec_count), jnp.float32),
@@ -372,17 +374,18 @@
         omega.reshape(blocks, pair_block),
         table,
     )
-    projected, basis = pl.pallas_call(
+    sigma, projected, basis = pl.pallas_call(
         functools.partial(basis_kernel, row_count * n_blk * n_col),
         out_shape=(
+            jax.ShapeDtypeStruct((row_count, vec_count), jnp.bfloat16),
             jax.ShapeDtypeStruct((vec_count, vec_count), jnp.float32),
             jax.ShapeDtypeStruct((row_count, vec_count), jnp.float32),
         ),
         in_specs=[vmem] * 3,
-        out_specs=(vmem, vmem),
+        out_specs=(vmem, vmem, vmem),
         compiler_params=pltpu.CompilerParams(vmem_limit_bytes=60 << 20),
         name="basis",
-    )(sums, trial, sigma)
+    )(sums, trial, coupled)
     return (sigma, projected, basis)
 
 

time: 60.3 us -> 57.7 us (0.957)
  local copies, waits for them, and re-layouts: 1.67 us -> 0 us
  Pallas kernels: 57.8 us -> 56.9 us
    unnamed x1 -> x0, local copies, waits for them, and re-layouts: 1.67 us -> none
    pallas_call x1, Pallas kernels: 50.4 us -> 49.5 us  [on_device(): pl.pallas_call(functools.partial(couple_kernel, n_blk, n_col, near), out_...]
where the time goes in v3:
time: 57.7 us; the launch traced here: 57.5 us
  Pallas kernels  56.9 us (99%)
  between operations  0.64 us (1%)
    pallas_call x1, Pallas kernels, on_device(): pl.pallas_call(functools.partial(couple_kernel, n_blk, n_col, near), out_...  49.5 us
    pallas_call x1, Pallas kernels, on_device(): pl.pallas_call(functools.partial(basis_kernel, row_count * n_blk * n_col)...  7.42 us

profile of v3, /device:TPU:0, one launch (start us, length us, event | category | flops | bytes accessed | tf_op | source)
XLA Modules:
  0.0 57.5 jit_solution(7690766390436933205)
XLA Ops:
  0.6 49.5 %couple.1 = (bf16[1024,128]{1,0:T(8,128)(2,1)}, f32[384,128]{1,0:T(8,128)}) custom-call(s32[8,72]{1,0:T(8,128)} %kinds_ref.1, s32[8,72]{1,0:T(8,128)} %cycle_ref.1, s32[8,72]{1,0:T(8,128)} %source_ref.1, bf16[8,128,128]{2,1,0:T(8,128)(2,1)} %bitcast.2, f32[8,128]{1,0:T(8,128)} %bitcast.3, bf16[64,128,128]{2,1,0:T(8,128)(2,1)} %table_hbm.1), custom_call_target="tpu_custom_call" | custom-call | tf_op jit(solution)/shard_map/couple/pallas_call | solution.py:338
  50.1 7.4 %basis.1 = (bf16[1024,128]{1,0:T(8,128)(2,1)}, f32[128,128]{1,0:T(8,128)}, f32[1024,128]{1,0:T(8,128)}) custom-call(f32[384,128]{1,0:T(8,128)} %get-tuple-element.5.sums_ref, bf16[1024,128]{1,0:T(8,128)(2,1)} %trial_ref.1, bf16[1024,128]{1,0:T(8,128)(2,1)} %get-tuple-element.6.coupled_ref), custom_call_target="tpu_custom_call" | custom-call | tf_op jit(solution)/shard_map/basis/pallas_call | solution.py:377

commit v4 on v3

--- a/solution.py
+++ b/solution.py
@@ -100,8 +100,15 @@
         )
 
     for h in halves:
-        to_up[h].start()
-        to_down[h].start()
+
+        @pl.when(high != far - 1)
+        def _():
+            to_up[h].start()
+
+        @pl.when(high != 0)
+        def _():
+            to_down[h].start()
+
         own_x[h].start()
         own_y[h].start()
 
@@ -113,6 +120,15 @@
     for h in halves:
         own_x[h].wait_recv()
         pass_y[h].start()
+
+        @pl.when(high == far - 1)
+        def _():
+            to_up[h].start()
+
+        @pl.when(high == 0)
+        def _():
+            to_down[h].start()
+
     for h in halves:
         far_arrival(x, h).wait_recv()
         far_x[h].start()
@@ -138,9 +154,6 @@
         pass_y[h].wait_recv()
         far_x[h].wait_recv()
         pass_x[h].wait_recv()
-    for sent in (to_up, to_down, own_x, own_y, pass_y, far_x, far_y, pass_x):
-        for h in halves:
-            sent[h].wait_send()
 
     chunk = max(size for size in range(1, 9) if per_row % size == 0)
     row_id = lax.broadcasted_iota(jnp.int32, (pair_block, pair_block), 0)
@@ -167,6 +180,9 @@
         return carry
 
     lax.fori_loop(0, blocks, one_block, 0)
+    for sent in (to_up, to_down, own_x, own_y, pass_y, far_x, far_y, pass_x):
+        for h in halves:
+            sent[h].wait_send()
 
     sigma = sigma_ref[...]
     both = jnp.concatenate([across[...], sigma.T], axis=0)

time: 57.7 us -> 57.4 us (level)
  no operation moved by 1% of the time
where the time goes in v4:
time: 57.4 us; the launch traced here: 57.2 us
  Pallas kernels  56.6 us (99%)
  between operations  0.64 us (1%)
    pallas_call x1, Pallas kernels, on_device(): pl.pallas_call(functools.partial(couple_kernel, n_blk, n_col, near), out_...  49.1 us
    pallas_call x1, Pallas kernels, on_device(): pl.pallas_call(functools.partial(basis_kernel, row_count * n_blk * n_col)...  7.42 us

profile of v4, /device:TPU:0, one launch (start us, length us, event | category | flops | bytes accessed | tf_op | source)
XLA Modules:
  0.0 57.2 jit_solution(11217264841204239787)
XLA Ops:
  0.6 49.1 %couple.1 = (bf16[1024,128]{1,0:T(8,128)(2,1)}, f32[384,128]{1,0:T(8,128)}) custom-call(s32[8,72]{1,0:T(8,128)} %kinds_ref.1, s32[8,72]{1,0:T(8,128)} %cycle_ref.1, s32[8,72]{1,0:T(8,128)} %source_ref.1, bf16[8,128,128]{2,1,0:T(8,128)(2,1)} %bitcast.2, f32[8,128]{1,0:T(8,128)} %bitcast.3, bf16[64,128,128]{2,1,0:T(8,128)(2,1)} %table_hbm.1), custom_call_target="tpu_custom_call" | custom-call | tf_op jit(solution)/shard_map/couple/pallas_call | solution.py:354
  49.8 7.4 %basis.1 = (bf16[1024,128]{1,0:T(8,128)(2,1)}, f32[128,128]{1,0:T(8,128)}, f32[1024,128]{1,0:T(8,128)}) custom-call(f32[384,128]{1,0:T(8,128)} %get-tuple-element.5.sums_ref, bf16[1024,128]{1,0:T(8,128)(2,1)} %trial_ref.1, bf16[1024,128]{1,0:T(8,128)(2,1)} %get-tuple-element.6.coupled_ref), custom_call_target="tpu_custom_call" | custom-call | tf_op jit(solution)/shard_map/basis/pallas_call | solution.py:393
